TPU v7x, 512 devices: a whole 4x4x16 slice. The times are simulated.
512 devices in a mesh: cell: 32 (over z_lo, x, core), feat: 16 (over z_hi, y).
Axes of the slice: x: 4, y: 4, z: 16 (z_hi: 4, z_lo: 4; z = z_hi * 4 + z_lo), core: 2. Of those that a mesh axis runs over, the one named last changes fastest.
Arguments:
- rna_counts: bfloat16 [65536, 4096], P('cell', 'feat'), may hold values from -6 to 6
- rna_embed: bfloat16 [65536, 64], P('cell'), may hold values from -3 to 3
- rna_potential: float32 [65536], P('cell'), may hold values from -1 to 1
- atac_counts: bfloat16 [16384, 16384], P('feat', 'cell'), may hold values from -6 to 6
- atac_embed: bfloat16 [16384, 64], P('feat'), may hold values from -3 to 3
- atac_potential: bfloat16 [16384], P('feat'), may hold values from -1 to 1
- panel_ids: int32 [1024], P('feat'), may hold values from 0 to 16383, as said below
Outputs:
- feature_cross: bfloat16 [4096, 16384], P('feat', 'cell')
- gene_term: float32 [4096], P('feat')
- peak_term: float32 [16384], P('cell')
Inputs may be any that keep to these rules, and one draw needn't show every extreme that they name: `panel_ids`: the ids in slots k * 64 to (k + 1) * 64 - 1 are distinct and lie among ATAC cells k * 1024 to (k + 1) * 1024 - 1.
All inputs are finite; a program needn't handle non-finite values.
Results may differ from a plain program's by a relative error of at most 0.0058.
Values may be sent and summed in bfloat16 or wider, within the bound.
A program may use at most 64 MiB of HBM per device.

v0:
```python
import math
import jax
import jax.numpy as jnp
from jax import lax
from jax.sharding import PartitionSpec as P


def local(rna_counts, rna_embed, rna_potential, atac_counts, atac_embed, atac_potential, panel_ids):
    owner = lax.axis_index("feat")
    local_ids = panel_ids - owner * atac_counts.shape[0]
    chosen_rows = jnp.take(atac_counts, local_ids, axis=0)
    chosen_embed = jnp.take(atac_embed, local_ids, axis=0)
    chosen_potential = jnp.take(atac_potential, local_ids, axis=0)
    panel_rows, panel_embed, panel_potential = (
        lax.all_gather(chosen_rows, "feat", axis=0, tiled=True),
        lax.all_gather(chosen_embed, "feat", axis=0, tiled=True),
        lax.all_gather(chosen_potential, "feat", axis=0, tiled=True),
    )
    panel_float = panel_potential.astype(jnp.float32)
    inverse = 1.0 / math.sqrt(rna_embed.shape[1])
    rows_here = rna_counts.shape[0]
    genes_here = rna_counts.shape[1]
    panel_size = panel_embed.shape[0]
    height = min(512, rows_here)
    number = rows_here // height
    items = (
        rna_counts.reshape(number, height, genes_here),
        rna_embed.reshape(number, height, rna_embed.shape[1]),
        rna_potential.reshape(number, height),
    )

    def advance(carry, item):
        total, gene_sum, panel_mass = carry
        block_rows, block_embed, block_potential = item
        score = lax.dot_general(
            block_embed, panel_embed, (((1,), (1,)), ((), ())), preferred_element_type=jnp.float32
        )
        coupling = jnp.exp(
            block_potential[:, None] + panel_float[None, :] + score * inverse
        ).astype(jnp.bfloat16)
        widened = coupling.astype(jnp.float32)
        row_mass = jnp.sum(widened, axis=1)
        panel_mass = panel_mass + jnp.sum(widened, axis=0)
        total = total + lax.dot_general(
            block_rows, coupling, (((0,), (0,)), ((), ())), preferred_element_type=jnp.float32
        )
        squares = jnp.square(block_rows.astype(jnp.float32))
        gene_sum = gene_sum + jnp.dot(row_mass, squares, precision=lax.Precision.HIGHEST)
        return ((total, gene_sum, panel_mass), None)

    start = (
        jnp.zeros((genes_here, panel_size), jnp.float32),
        jnp.zeros((genes_here,), jnp.float32),
        jnp.zeros((panel_size,), jnp.float32),
    )
    (total, gene_sum, panel_mass), unused = lax.scan(advance, start, items)
    total, gene_sum, panel_mass = lax.psum((total, gene_sum, panel_mass), "cell")
    reduced = total.astype(jnp.bfloat16)
    all_rows = rows_here * lax.axis_size("cell")
    scale = 1.0 / math.sqrt(all_rows * panel_size)
    mass_scale = 1.0 / (all_rows * panel_size)
    feature_cross = (
        jnp.dot(reduced, panel_rows, preferred_element_type=jnp.float32) * scale
    ).astype(jnp.bfloat16)
    gene_term = gene_sum * mass_scale
    peak_term = (
        jnp.dot(
            panel_mass, jnp.square(panel_rows.astype(jnp.float32)), precision=lax.Precision.HIGHEST
        )
        * mass_scale
    )
    return (feature_cross, gene_term, peak_term)


def solution(mesh):
    placed = (
        P("cell", "feat"),
        P("cell", None),
        P("cell"),
        P("feat", "cell"),
        P("feat", None),
        P("feat"),
        P("feat"),
    )
    return jax.shard_map(
        local,
        mesh=mesh,
        in_specs=placed,
        out_specs=(P("feat", "cell"), P("feat"), P("cell")),
        check_vma=False,
    )
```

profile of v0, /device:TPU:8, one launch (start us, length us, event | category | flops | bytes accessed | tf_op | source)
XLA Modules:
  0.0 298.3 jit_solution(12561693052006271583)
XLA Ops:
  7.3 0.7 compare_and_fusion
  8.4 0.7 gather_fusion.2
  9.1 0.7 broadcast_select_fusion
  9.9 0.8 gather_fusion
  10.7 1.3 dynamic-slice
  12.9 52.7 %all-reduce = bf16[1024]{0:T(1024)(128)(2,1)S(1)} all-reduce(bf16[1024]{0:T(1024)(128)(2,1)S(1)} %dynamic-update-slice), channel_id=1, replica_groups=mesh['cell'=32,'feat'=16] {'feat'}, use_global_device_ids=true, to_apply=%add | all-reduce | flops 1024 | bytes 4096
  66.5 54.9 %all_gather.10 = bf16[1024,64]{1,0:T(8,128)(2,1)S(1)} all-gather(bf16[64,64]{1,0:T(8,128)(2,1)S(1)} %broadcast_select_fusion.1), channel_id=1, replica_groups=mesh['cell'=32,'feat'=16] {'feat'}, dimensions={0}, use_global_device_ids=true | all-gather | bytes 139264 | tf_op jit(solution)/shard_map/all_gather | solution.py:16
  121.3 1.0 copy.12
  122.4 18.1 %while.15 = (s32[]{:T(128)}, f32[256,1024]{1,0:T(8,128)S(1)}, f32[256]{0:T(256)S(1)}, f32[1024]{0:T(1024)S(1)}, bf16[4,512,256]{2,1,0:T(8,128)(2,1)}, /*index=5*...) while((s32[]{:T(128)}, f32[256,1024]{1,0:T(8,128)S(1)}, ...), condition=%wide.region_3.4_spmd.clone, body=%wide.region_0.3_spmd.clone.sunk | while | flops 341574656 | bytes 5017213 | solution.py:56
  122.4 1.7 convert_reduce_fusion.3
  124.0 1.5 convolution_add_fusion.2
  125.5 1.3 fusion.34
  126.9 1.7 convert_reduce_fusion.3
  128.6 1.5 convolution_add_fusion.2
  130.1 1.3 fusion.34
  131.4 1.7 convert_reduce_fusion.3
  133.1 1.5 convolution_add_fusion.2
  134.6 1.3 fusion.34
  136.0 1.7 convert_reduce_fusion.3
  137.6 1.5 convolution_add_fusion.2
  139.1 1.3 fusion.34
  140.5 146.1 %all-reduce.3 = (bf16[256,1024]{1,0:T(8,128)(2,1)S(1)}, f32[256]{0:T(256)S(1)}, f32[1024]{0:T(1024)S(1)}) all-reduce(f32[256,1024]{1,0:T(8,128)S(1)} %get-tuple-element.52, f32[256]{0:T(256)S(1)} %get-tuple-element.53, f32[1024]{0:T(1024)S(1)} %get-tuple-element.54), channel_id=1, replica_groups=mesh['cell'=32,'feat'=16] {'cell'}, use_global_device_ids=true, to_apply=%region_4.5 | all-reduce | flops 263424 | bytes 1583104 | tf_op jit(solution)/shard_map/psum | solution.py:57
  287.2 2.5 fusion.12
  290.3 1.1 fusion.15
  (41 shorter events, 3.0 us)
Async XLA Ops:
  7.2 1.2 copy-start
  7.2 2.7 copy-start.1
  7.2 58.4 %copy-start.4 = (bf16[1024,64]{0,1:T(8,128)(2,1)S(1)}, bf16[1024,64]{0,1:T(8,128)(2,1)}, u32[]{:S(2)}) copy-start(bf16[1024,64]{0,1:T(8,128)(2,1)} %param.13) | copy-start | bytes 393220
  7.2 280.0 %all-gather.2.cloned.1.call-start = ((), (), s32[]{:S(2)}) async-start(), calls=%async_computation | async-start | bytes 1114112 | tf_op jit(solution)/shard_map/all_gather | solution.py:15
  8.4 112.9 %copy-start.3 = (bf16[2048,64]{0,1:T(8,128)(2,1)S(1)}, bf16[2048,64]{0,1:T(8,128)(2,1)}, u32[]{:S(2)}) copy-start(bf16[2048,64]{0,1:T(8,128)(2,1)} %param.10) | copy-start | bytes 786436
  9.9 112.5 %copy-start.5 = (f32[2048]{0:T(1024)S(1)}, f32[2048]{0:T(1024)}, u32[]{:S(2)}) copy-start(f32[2048]{0:T(1024)} %param.11) | copy-start | bytes 24580
  287.2 3.1 %copy-start.2 = (bf16[1024,512]{1,0:T(8,128)(2,1)S(1)}, bf16[1024,512]{1,0:T(8,128)(2,1)}, u32[]{:S(2)}) copy-start(bf16[1024,512]{1,0:T(8,128)(2,1)} %all-gather.2.cloned.1.call-done) | copy-start | bytes 3145732
Sparse Core Ops, SparseCore 0:
  11.6 81.7 all-gather.1
where the time goes:
time: 299 us; the launch traced here: 298 us
  blocking collectives  254 us (85%)
  matrix products  21.4 us (7%)
  between operations  14.8 us (5%)
  local copies, waits for them, and re-layouts  5.31 us (2%)
    psum x1, blocking collectives, local(): lax.psum((total, gene_sum, panel_mass), 'cell')  146 us
    all_gather x1, blocking collectives, local(): lax.all_gather(chosen_embed, 'feat', axis=0, tiled=True)  54.9 us
    unnamed x1, blocking collectives  52.7 us
    dot_general x4, matrix products, advance(): lax.dot_general(block_embed, panel_embed, (((1,), (1,)), ((), ())), prefe...  6.7 us
  transfers between devices with their start and end apart: 1, of which 0 were waited for; matrix products, arithmetic and copies ran while one was open for 8% of the time, Pallas kernels for 0%

commit v1 on v0

--- a/solution.py
+++ b/solution.py
@@ -11,9 +11,13 @@
     chosen_rows = jnp.take(atac_counts, local_ids, axis=0)
     chosen_embed = jnp.take(atac_embed, local_ids, axis=0)
     chosen_potential = jnp.take(atac_potential, local_ids, axis=0)
+    register_modes_here = lambda work_x, k_dim: jnp.concatenate(
+        lax.all_to_all(jnp.stack([work_x for _ in range(lax.axis_size("feat"))]), "feat", 0, 0),
+        k_dim,
+    )
     panel_rows, panel_embed, panel_potential = (
         lax.all_gather(chosen_rows, "feat", axis=0, tiled=True),
-        lax.all_gather(chosen_embed, "feat", axis=0, tiled=True),
+        register_modes_here(chosen_embed, 0),
         lax.all_gather(chosen_potential, "feat", axis=0, tiled=True),
     )
     panel_float = panel_potential.astype(jnp.float32)

time: 299 us -> 260 us (0.87)
  blocking collectives: 254 us -> 195 us
  starting transfers between devices: 0.04 us -> 18.2 us
    all_gather x1 -> x0, blocking collectives: 54.9 us -> none  [local(): lax.all_gather(chosen_embed, 'feat', axis=0, tiled=True)]
    all_to_all x0 -> x1, starting transfers between devices: none -> 18.2 us  [local(): lax.all_to_all(jnp.stack([work_x for _ in range(lax.axis_size('feat'))]),...]
    unnamed x1, blocking collectives: 52.7 us -> 47.2 us
  transfers between devices with their start and end apart: 1 -> 2, of which waited for: 0 -> 0; matrix products, arithmetic and copies ran while one was open for 8% -> 9% of each run, Pallas kernels for 0% -> 0%
where the time goes in v1:
time: 260 us; the launch traced here: 259 us
  blocking collectives  195 us (75%)
  matrix products  21.4 us (8%)
  starting transfers between devices  18.2 us (7%)
  between operations  14.8 us (6%)
  local copies, waits for them, and re-layouts  6.95 us (3%)
  other arithmetic  2.91 us (1%)
    psum x1, blocking collectives, local(): lax.psum((total, gene_sum, panel_mass), 'cell')  148 us
    unnamed x1, blocking collectives  47.2 us
    all_to_all x1, starting transfers between devices, local(): lax.all_to_all(jnp.stack([work_x for _ in range(lax.axis_size('feat'))]),...  18.2 us
    dot_general x4, matrix products, advance(): lax.dot_general(block_embed, panel_embed, (((1,), (1,)), ((), ())), prefe...  6.7 us
    dot_general x4, matrix products, advance(): lax.dot_general(block_rows, coupling, (((0,), (0,)), ((), ())), preferred...  5.96 us
  transfers between devices with their start and end apart: 2, of which 0 were waited for; matrix products, arithmetic and copies ran while one was open for 9% of the time, Pallas kernels for 0%

profile of v1, /device:TPU:8, one launch (start us, length us, event | category | flops | bytes accessed | tf_op | source)
XLA Modules:
  0.0 259.2 jit_solution(2083175445968312489)
XLA Ops:
  7.2 0.8 compare_and_fusion
  7.9 1.1 copy.13
  9.8 0.9 reshape.74
  10.7 18.2 %all-to-all-start = ((bf16[16,2,2048]{2,1,0:T(2,128)(2,1)}), bf16[16,2,2048]{2,1,0:T(2,128)(2,1)S(1)}, u32[]{:S(2)}, u32[]{:S(2)}) async-start(bf16[16,2,2048]{2,1,0:T(2,128)(2,1)} %reshape.74), calls=%async_computation | async-start | bytes 262144 | tf_op jit(solution)/shard_map/all_to_all | solution.py:15
  30.4 0.8 gather_fusion
  31.2 1.3 dynamic-slice
  33.4 47.2 %all-reduce = bf16[1024]{0:T(1024)(128)(2,1)S(1)} all-reduce(bf16[1024]{0:T(1024)(128)(2,1)S(1)} %dynamic-update-slice), channel_id=1, replica_groups=mesh['cell'=32,'feat'=16] {'feat'}, use_global_device_ids=true, to_apply=%add | all-reduce | flops 1024 | bytes 4096
  80.6 1.0 copy.12
  81.8 18.1 %while.15 = (s32[]{:T(128)}, f32[256,1024]{1,0:T(8,128)S(1)}, f32[256]{0:T(256)S(1)}, f32[1024]{0:T(1024)S(1)}, bf16[4,512,256]{2,1,0:T(8,128)(2,1)}, /*index=5*...) while((s32[]{:T(128)}, f32[256,1024]{1,0:T(8,128)S(1)}, ...), condition=%wide.region_3.4_spmd.clone, body=%wide.region_0.3_spmd.clone.sunk | while | flops 341574656 | bytes 5017213 | solution.py:60
  81.9 1.7 convert_reduce_fusion.3
  83.6 1.5 convolution_add_fusion.2
  85.0 1.3 fusion.34
  86.4 1.7 convert_reduce_fusion.3
  88.1 1.5 convolution_add_fusion.2
  89.6 1.3 fusion.34
  90.9 1.7 convert_reduce_fusion.3
  92.6 1.5 convolution_add_fusion.2
  94.1 1.3 fusion.34
  95.5 1.7 convert_reduce_fusion.3
  97.2 1.5 convolution_add_fusion.2
  98.7 1.3 fusion.34
  100.0 147.5 %all-reduce.3 = (bf16[256,1024]{1,0:T(8,128)(2,1)S(1)}, f32[256]{0:T(256)S(1)}, f32[1024]{0:T(1024)S(1)}) all-reduce(f32[256,1024]{1,0:T(8,128)S(1)} %get-tuple-element.52, f32[256]{0:T(256)S(1)} %get-tuple-element.53, f32[1024]{0:T(1024)S(1)} %get-tuple-element.54), channel_id=1, replica_groups=mesh['cell'=32,'feat'=16] {'cell'}, use_global_device_ids=true, to_apply=%region_4.5 | all-reduce | flops 263424 | bytes 1583104 | tf_op jit(solution)/shard_map/psum | solution.py:61
  248.1 2.5 fusion.12
  251.2 1.1 fusion.15
  (43 shorter events, 4.1 us)
Async XLA Ops:
  7.2 21.8 %copy-start = (bf16[1024,512]{1,0:T(8,128)(2,1)S(1)}, bf16[1024,512]{1,0:T(8,128)(2,1)}, u32[]{:S(2)}) copy-start(bf16[1024,512]{1,0:T(8,128)(2,1)} %param.12) | copy-start | bytes 3145732
  9.0 21.4 %copy-start.1 = (bf16[1024]{0:T(1024)(128)(2,1)S(1)}, bf16[1024]{0:T(1024)(128)(2,1)}, u32[]{:S(2)}) copy-start(bf16[1024]{0:T(1024)(128)(2,1)} %param.14) | copy-start | bytes 6148
  9.8 70.8 %copy-start.3 = (bf16[2048,64]{0,1:T(8,128)(2,1)S(1)}, bf16[2048,64]{0,1:T(8,128)(2,1)}, u32[]{:S(2)}) copy-start(bf16[2048,64]{0,1:T(8,128)(2,1)} %param.10) | copy-start | bytes 786436
  10.7 70.9 %all-to-all-start = ((bf16[16,2,2048]{2,1,0:T(2,128)(2,1)}), bf16[16,2,2048]{2,1,0:T(2,128)(2,1)S(1)}, u32[]{:S(2)}, u32[]{:S(2)}) async-start(bf16[16,2,2048]{2,1,0:T(2,128)(2,1)} %reshape.74), calls=%async_computation | async-start | bytes 262144 | tf_op jit(solution)/shard_map/all_to_all | solution.py:15
  28.9 52.7 %copy-start.4 = (f32[2048]{0:T(1024)S(1)}, f32[2048]{0:T(1024)}, u32[]{:S(2)}) copy-start(f32[2048]{0:T(1024)} %param.11) | copy-start | bytes 24580
  28.9 219.2 %all-gather.2.cloned.1.call-start = ((), (), s32[]{:S(2)}) async-start(), calls=%async_computation.1 | async-start | bytes 1114112 | tf_op jit(solution)/shard_map/all_gather | solution.py:19
  248.1 3.1 %copy-start.2 = (bf16[1024,512]{1,0:T(8,128)(2,1)S(1)}, bf16[1024,512]{1,0:T(8,128)(2,1)}, u32[]{:S(2)}) copy-start(bf16[1024,512]{1,0:T(8,128)(2,1)} %all-gather.2.cloned.1.call-done) | copy-start | bytes 3145732
Sparse Core Ops, SparseCore 0:
  32.7 78.3 all-gather.1
